TPU v7x, 256 devices: a whole 4x4x8 slice. The times are simulated.
256 devices in a mesh: row: 32 (over z_lo, y, core), col: 8 (over z_hi, x).
Axes of the slice: x: 4, y: 4, z: 8 (z_hi: 2, z_lo: 4; z = z_hi * 4 + z_lo), core: 2. Of those that a mesh axis runs over, the one named last changes fastest.
Arguments:
- slab: bfloat16 [32768, 16384], P('row', 'col'), may hold values from -6 to 6
- panel_left: bfloat16 [32768, 512], P('row', 'col'), may hold values from -3 to 3
- panel_top: bfloat16 [512, 16384], P('row', 'col'), may hold values from -3 to 3
- row_bases: bfloat16 [32768, 256], P('row'), may hold values from -0.25 to 0.25
- col_bases: bfloat16 [16384, 256], P('col'), may hold values from -0.25 to 0.25
- row_ranks: int32 [64], P('row'), may hold values from 32 to 256, as said below
- col_ranks: int32 [32], P('col'), may hold values from 32 to 256, as said below
- pivot_inverse: bfloat16 [512, 512], replicated, may hold values from -0.0625 to 0.0625
- pivot_rhs: bfloat16 [512, 4096], P('row', 'col'), may hold values from -6 to 6
- rhs: bfloat16 [32768, 4096], P('row', 'col'), may hold values from -6 to 6
Outputs:
- slab_new: bfloat16 [32768, 16384], P('row', 'col')
- rhs_new: bfloat16 [32768, 4096], P('row', 'col')
Inputs may be any that keep to these rules, and one draw needn't show every extreme that they name: `row_ranks`: each entry is the rank of one tile; the value 256 occurs in every draw. `col_ranks`: each entry is the rank of one tile; the value 256 occurs in every draw.
All inputs are finite; a program needn't handle non-finite values.
Results may differ from a plain program's by a relative error of at most 0.0062.
Values may be sent and summed in bfloat16 or wider, within the bound.
No kernel may reach another device: no remote copies, remote signals or barrier semaphores. Data moves between devices by JAX's collectives and lax.ppermute only.
A program may use at most 128 MiB of HBM per device.

v0:
```python
import jax
import jax.numpy as jnp
from jax import lax
from jax.sharding import PartitionSpec as P


def from_everyone(array, axis):
    copies = jnp.broadcast_to(array, (lax.axis_size(axis), *array.shape))
    return lax.all_to_all(copies, axis, split_axis=0, concat_axis=0, tiled=True)


def joined_along(blocks, dim):
    blocks = jnp.moveaxis(blocks, 0, dim)
    lengths = blocks.shape
    return blocks.reshape(*lengths[:dim], lengths[dim] * lengths[dim + 1], *lengths[dim + 2 :])


def gather_directly(array, axis, dim):
    blocks = from_everyone(array, axis)
    return joined_along(blocks, dim)


def per_device(
    slab,
    panel_left,
    panel_top,
    row_bases,
    col_bases,
    row_ranks,
    col_ranks,
    pivot_inverse,
    pivot_rhs,
    rhs,
):
    tile_order = pivot_inverse.shape[0]
    rank_width = row_bases.shape[1]
    row_count = row_ranks.shape[0]
    column_count = col_ranks.shape[0]
    gain_width = rhs.shape[1]
    levels = jnp.arange(rank_width, dtype=jnp.int32)
    keep_row = (levels[None, :] < row_ranks[:, None]).astype(jnp.float32)
    keep_column = (levels[None, :] < col_ranks[:, None]).astype(jnp.float32)
    left_bases = row_bases.reshape(row_count, tile_order, rank_width)
    right_bases = col_bases.reshape(column_count, tile_order, rank_width)
    left_tiles = panel_left.reshape(row_count, tile_order, panel_left.shape[1])
    part_core = jnp.einsum(
        "tbr,tbc->trc", left_bases, left_tiles, preferred_element_type=jnp.float32
    )
    part_core = (part_core * keep_row[:, :, None]).astype(jnp.bfloat16)
    row_core = gather_directly(part_core, "col", 2)
    shaped = panel_top.reshape(panel_top.shape[0], column_count, tile_order)
    projected = jnp.einsum("pjc,jcr->pjr", shaped, right_bases, preferred_element_type=jnp.float32)
    outgoing = (projected * keep_column[None]).astype(jnp.bfloat16)
    arrived, rhs_rows = (
        lax.all_gather(outgoing, "row", axis=0, tiled=True),
        lax.all_gather(pivot_rhs, "row", axis=0, tiled=True),
    )
    solved = jnp.dot(pivot_inverse, rhs_rows, preferred_element_type=jnp.float32)
    core_block = jnp.einsum(
        "irp,pjs->ijrs", row_core, arrived, preferred_element_type=jnp.float32
    ).astype(jnp.bfloat16)
    spread = jnp.einsum(
        "ibr,ijrs->ijbs", left_bases, core_block, preferred_element_type=jnp.float32
    ).astype(jnp.bfloat16)
    change = jnp.einsum("ijbs,jcs->ibjc", spread, right_bases, preferred_element_type=jnp.float32)
    change = change.reshape(row_count * tile_order, column_count * tile_order)
    slab_new = (slab.astype(jnp.float32) - change).astype(jnp.bfloat16)
    pivot_solution = solved.astype(jnp.bfloat16)
    reduced = jnp.einsum(
        "irp,pg->irg", row_core, pivot_solution, preferred_element_type=jnp.float32
    ).astype(jnp.bfloat16)
    lowered = jnp.einsum("ibr,irg->ibg", left_bases, reduced, preferred_element_type=jnp.float32)
    lowered = lowered.reshape(row_count * tile_order, gain_width)
    rhs_new = (rhs.astype(jnp.float32) - lowered).astype(jnp.bfloat16)
    return (slab_new, rhs_new)


def solution(mesh):
    in_specs = (
        P("row", "col"),
        P("row", "col"),
        P("row", "col"),
        P("row", None),
        P("col", None),
        P("row"),
        P("col"),
        P(),
        P("row", "col"),
        P("row", "col"),
    )
    out_specs = (P("row", "col"), P("row", "col"))
    return jax.shard_map(
        per_device, mesh=mesh, in_specs=in_specs, out_specs=out_specs, check_vma=False
    )
```

profile of v0, /device:TPU:1, one launch (start us, length us, event | category | flops | bytes accessed | tf_op | source)
XLA Modules:
  0.0 118.2 jit_solution(15169704312447534713)
XLA Ops:
  7.2 0.0 copy-start
  7.2 0.0 copy-start.2
  7.2 0.0 all-gather.2.cloned.1.call-start
  7.2 0.8 fusion.16
  8.1 0.3 copy-done
  8.4 1.1 fusion.10
  9.5 0.6 copy.17
  10.1 0.0 all-gather.2.cloned.1.call-update
  10.1 0.7 compare_convert_fusion
  10.9 1.3 %fusion.8 = bf16[2,256,64]{1,2,0:T(8,128)(2,1)S(1)} fusion(bf16[2,512,256]{2,1,0:T(8,128)(2,1)} %bitcast.57, bf16[8,2,8,512]{3,2,1,0:T(8,128)(2,1)} %bitcast.62, f32[2,256]{1,0:T(2,128)S(1)} %compare_convert_fusion), kind=kOutput, calls=%fused_computation.14 | convolution fusion | flops 33619968 | bytes 722944 | tf_op jit(solution)/shard_map/tbr,tbc->trc/dot_general | solution.py:46
  12.2 0.8 broadcast_in_dim.2
  13.0 11.5 %all-to-all-start = ((bf16[8,2,256,64]{2,3,1,0:T(8,128)(2,1)}), bf16[8,2,256,64]{2,3,1,0:T(8,128)(2,1)S(1)}, u32[]{:S(2)}, u32[]{:S(2)}) async-start(bf16[8,2,256,64]{2,3,1,0:T(8,128)(2,1)} %broadcast_in_dim.2), calls=%async_computation | async-start | bytes 1048576 | tf_op jit(solution)/shard_map/all_to_all | solution.py:9
  24.5 46.1 %all_gather.7 = bf16[512,512]{1,0:T(8,128)(2,1)S(1)} all-gather(bf16[16,512]{1,0:T(8,128)(2,1)} %param.18), channel_id=1, replica_groups=mesh['row'=32,'col'=8] {'row'}, dimensions={0}, use_global_device_ids=true | all-gather | bytes 540672 | tf_op jit(solution)/shard_map/all_gather | solution.py:56
  70.6 0.0 copy-done.2
  70.6 1.3 %fusion.6 = bf16[512,512,1]{1,0,2:T(8,128)(2,1)} fusion(bf16[512,512]{1,0:T(8,128)(2,1)S(1)} %copy-done.2, bf16[512,512]{1,0:T(8,128)(2,1)S(1)} %all_gather.7), kind=kOutput, calls=%fused_computation.11 | convolution fusion | flops 268697600 | bytes 1572864 | tf_op jit(solution)/shard_map/dot_general | solution.py:58
  71.9 0.0 all-to-all-done
  71.9 0.8 copy.19
  72.7 2.2 %fusion.7 = f32[2,512,512]{1,2,0:T(8,128)S(1)} fusion(bf16[2,512,256]{2,1,0:T(8,128)(2,1)} %bitcast.58, bf16[2,256,512]{1,2,0:T(8,128)(2,1)} %bitcast.60, bf16[512,512,1]{1,0,2:T(8,128)(2,1)} %fusion.6), kind=kOutput, calls=%fused_computation.12 | convolution fusion | flops 537133056 | bytes 3670016 | tf_op jit(solution)/shard_map/ibr,irg->ibg/dot_general | solution.py:72
  74.9 2.7 %fusion = bf16[1024,512]{1,0:T(8,128)(2,1)} fusion(f32[2,512,512]{1,2,0:T(8,128)S(1)} %fusion.7, bf16[1024,512]{1,0:T(8,128)(2,1)} %param.19), kind=kLoop, calls=%fused_computation.3 | loop fusion | flops 1572864 | bytes 4194304 | tf_op jit(solution)/shard_map/convert_element_type | solution.py:74
  77.6 2.1 %all-gather.2.cloned.1.call-done = bf16[512,4,256]{2,1,0:T(4,128)(2,1)} async-done(((bf16[16,4,256]{2,1,0:T(4,128)(2,1)}), bf16[512,4,256]{2,1,0:T(4,128)(2,1)}) %all-gather.2.cloned.1.call-update) | async-done | bytes 1048592 | tf_op jit(solution)/shard_map/all_gather | solution.py:55
  79.8 2.1 %fusion.5 = bf16[2,4,256,256]{2,3,0,1:T(8,128)(2,1)S(1)} fusion(bf16[2,256,512,1]{1,2,0,3:T(8,128)(2,1)} %bitcast.61, bf16[512,4,256,1]{2,1,0,3:T(4,128)(2,1)} %bitcast.64), kind=kOutput, calls=%fused_computation.8 | convolution fusion | flops 537395200 | bytes 2621440 | tf_op jit(solution)/shard_map/irp,pjs->ijrs/dot_general | solution.py:59
  81.9 6.1 %convolution_bitcast_fusion = f32[2,512,4,512]{3,1,0,2:T(8,128)} fusion(bf16[4,512,256,1]{2,1,3,0:T(8,128)(2,1)S(1)} %bitcast.53, bf16[2,4,256,256]{2,3,0,1:T(8,128)(2,1)S(1)} %fusion.5, bf16[2,512,256,1]{2,1,0,3:T(8,128)(2,1)} %bitcast.59), kind=kOutput, calls=%fused_computation.1 | convolution fusion | flops 1611661312 | bytes 11010048 | tf_op jit(solution)/shard_map/ijbs,jcs->ibjc/dot_general | solution.py:65
  88.0 12.0 %copy.23 = f32[2,512,4,512]{3,2,1,0:T(4,128)} copy(f32[2,512,4,512]{3,1,0,2:T(8,128)} %convolution_bitcast_fusion) | data formatting | bytes 16777216 | tf_op jit(solution)/shard_map/ijbs,jcs->ibjc/transpose | solution.py:65
  100.0 0.0 copy-start.1
  100.0 7.8 %copy.35 = f32[128,8,4,512]{3,1,2,0:T(8,128)S(1)} copy(f32[128,8,4,512]{3,2,1,0:T(4,128)} %bitcast.55) | data formatting | bytes 16777216
  107.8 0.0 copy-done.1
  107.8 3.5 %subtract_convert_fusion = bf16[1024,2048]{1,0:T(8,128)(2,1)} fusion(f32[1024,2048]{1,0:T(8,128)S(1)} %bitcast.56, bf16[1024,2048]{1,0:T(8,128)(2,1)S(1)} %copy-done.1), kind=kLoop, calls=%fused_computation | loop fusion | flops 6291456 | bytes 16777216 | tf_op jit(solution)/shard_map/convert_element_type | solution.py:67
Async XLA Ops:
  7.2 1.2 %copy-start = (bf16[2048,256]{1,0:T(8,128)(2,1)S(1)}, bf16[2048,256]{1,0:T(8,128)(2,1)}, u32[]{:S(2)}) copy-start(bf16[2048,256]{1,0:T(8,128)(2,1)} %param.14) | copy-start | bytes 3145732
  7.2 63.5 %copy-start.2 = (bf16[512,512]{1,0:T(8,128)(2,1)S(1)}, bf16[512,512]{1,0:T(8,128)(2,1)}, u32[]{:S(2)}) copy-start(bf16[512,512]{1,0:T(8,128)(2,1)} %param.17) | copy-start | bytes 1572868
  7.2 72.6 %all-gather.2.cloned.1.call-start = ((), (), s32[]{:S(2)}) async-start(), calls=%async_computation.1 | async-start | bytes 1081344 | tf_op jit(solution)/shard_map/all_gather | solution.py:55
  13.0 58.9 %all-to-all-start = ((bf16[8,2,256,64]{2,3,1,0:T(8,128)(2,1)}), bf16[8,2,256,64]{2,3,1,0:T(8,128)(2,1)S(1)}, u32[]{:S(2)}, u32[]{:S(2)}) async-start(bf16[8,2,256,64]{2,3,1,0:T(8,128)(2,1)} %broadcast_in_dim.2), calls=%async_computation | async-start | bytes 1048576 | tf_op jit(solution)/shard_map/all_to_all | solution.py:9
  100.0 7.9 %copy-start.1 = (bf16[1024,2048]{1,0:T(8,128)(2,1)S(1)}, bf16[1024,2048]{1,0:T(8,128)(2,1)}, u32[]{:S(2)}) copy-start(bf16[1024,2048]{1,0:T(8,128)(2,1)} %param.10) | copy-start | bytes 12582916
Sparse Core Ops, SparseCore 0:
  10.3 69.4 all-gather.1
where the time goes:
time: 119 us; the launch traced here: 118 us
  blocking collectives  46.1 us (39%)
  local copies, waits for them, and re-layouts  22.5 us (19%)
  matrix products  14.1 us (12%)
  between operations  14.1 us (12%)
  starting transfers between devices  11.5 us (10%)
  other arithmetic  7.77 us (7%)
  waiting for transfers between devices  2.16 us (2%)
    all_gather x1, blocking collectives, per_device(): lax.all_gather(pivot_rhs, 'row', axis=0, tiled=True)  46.1 us
    transpose x1, local copies, waits for them, and re-layouts, per_device(): jnp.einsum('ijbs,jcs->ibjc', spread, right_bases, preferred_element_type=...  12 us
    all_to_all x1, starting transfers between devices, from_everyone(): return lax.all_to_all(copies, axis, split_axis=0, concat_axis=0, tiled=True)  11.5 us
    unnamed x7, local copies, waits for them, and re-layouts  8.2 us
    dot_general x1, matrix products, per_device(): jnp.einsum('ijbs,jcs->ibjc', spread, right_bases, preferred_element_type=...  6.11 us
    convert_element_type x1, other arithmetic, per_device(): slab_new = (slab.astype(jnp.float32) - change).astype(jnp.bfloat16)  3.5 us
    convert_element_type x1, other arithmetic, per_device(): rhs_new = (rhs.astype(jnp.float32) - lowered).astype(jnp.bfloat16)  2.7 us
  transfers between devices with their start and end apart: 2, of which 1 were waited for; matrix products, arithmetic and copies ran while one was open for 8% of the time, Pallas kernels for 0%

commit v1 on v0

--- a/solution.py
+++ b/solution.py
@@ -2,6 +2,13 @@
 import jax.numpy as jnp
 from jax import lax
 from jax.sharding import PartitionSpec as P
+
+
+def swapped_in(value, axis, along):
+    size = lax.axis_size(axis)
+    parts = jnp.stack([value for _ in range(size)])
+    parts = lax.all_to_all(parts, axis, split_axis=0, concat_axis=0)
+    return jnp.concatenate(parts, axis=along)
 
 
 def from_everyone(array, axis):
@@ -53,7 +60,7 @@
     outgoing = (projected * keep_column[None]).astype(jnp.bfloat16)
     arrived, rhs_rows = (
         lax.all_gather(outgoing, "row", axis=0, tiled=True),
-        lax.all_gather(pivot_rhs, "row", axis=0, tiled=True),
+        swapped_in(pivot_rhs, "row", 0),
     )
     solved = jnp.dot(pivot_inverse, rhs_rows, preferred_element_type=jnp.float32)
     core_block = jnp.einsum(

time: 119 us -> 126 us (1.059)
  blocking collectives: 46.1 us -> 0 us
  waiting for transfers between devices: 2.16 us -> 40.7 us
  starting transfers between devices: 11.5 us -> 25.3 us
    all_gather x1 -> x0, blocking collectives: 46.1 us -> none  [per_device(): lax.all_gather(pivot_rhs, 'row', axis=0, tiled=True)]
    all_to_all x0 -> x1, waiting for transfers between devices: none -> 15.6 us  [swapped_in(): parts = lax.all_to_all(parts, axis, split_axis=0, concat_axis=0)]
    all_gather x1, waiting for transfers between devices: 2.14 us -> 16 us  [per_device(): lax.all_gather(outgoing, 'row', axis=0, tiled=True)]
    all_to_all x0 -> x1, starting transfers between devices: none -> 13.8 us  [swapped_in(): parts = lax.all_to_all(parts, axis, split_axis=0, concat_axis=0)]
    all_to_all x1, waiting for transfers between devices: 0.01 us -> 9.11 us  [from_everyone(): return lax.all_to_all(copies, axis, split_axis=0, concat_axis=0, tiled=True)]
    another operation x0 -> x1, local copies, waits for them, and re-layouts: none -> 1.57 us  [swapped_in(): parts = jnp.stack([value for _ in range(size)])]
  transfers between devices with their start and end apart: 2 -> 3, of which waited for: 1 -> 3; matrix products, arithmetic and copies ran while one was open for 8% -> 9% of each run, Pallas kernels for 0% -> 0%
where the time goes in v1:
time: 126 us
  waiting for transfers between devices  40.7 us (32%)
  starting transfers between devices  25.3 us (20%)
  local copies, waits for them, and re-layouts  23.7 us (19%)
  between operations  14.1 us (11%)
  matrix products  14 us (11%)
  other arithmetic  7.78 us (6%)
    all_gather x1, waiting for transfers between devices, per_device(): lax.all_gather(outgoing, 'row', axis=0, tiled=True)  16 us
    all_to_all x1, waiting for transfers between devices, swapped_in(): parts = lax.all_to_all(parts, axis, split_axis=0, concat_axis=0)  15.6 us
    all_to_all x1, starting transfers between devices, swapped_in(): parts = lax.all_to_all(parts, axis, split_axis=0, concat_axis=0)  13.8 us
    transpose x1, local copies, waits for them, and re-layouts, per_device(): jnp.einsum('ijbs,jcs->ibjc', spread, right_bases, preferred_element_type=...  12 us
    all_to_all x1, starting transfers between devices, from_everyone(): return lax.all_to_all(copies, axis, split_axis=0, concat_axis=0, tiled=True)  11.5 us
    all_to_all x1, waiting for transfers between devices, from_everyone(): return lax.all_to_all(copies, axis, split_axis=0, concat_axis=0, tiled=True)  9.11 us
    unnamed x7, local copies, waits for them, and re-layouts  7.86 us
    dot_general x1, matrix products, per_device(): jnp.einsum('ijbs,jcs->ibjc', spread, right_bases, preferred_element_type=...  6.1 us
  transfers between devices with their start and end apart: 3, of which 3 were waited for; matrix products, arithmetic and copies ran while one was open for 9% of the time, Pallas kernels for 0%

profile of v1, /device:TPU:1, one launch (start us, length us, event | category | flops | bytes accessed | tf_op | source)
XLA Modules:
  0.0 125.6 jit_solution(9886060214378824902)
XLA Ops:
  7.2 0.0 copy-start
  7.2 0.0 copy-start.2
  7.2 0.8 compare_convert_fusion
  8.0 1.3 %fusion.8 = bf16[2,256,64]{1,2,0:T(8,128)(2,1)S(1)} fusion(bf16[2,512,256]{2,1,0:T(8,128)(2,1)} %bitcast.58, bf16[8,2,8,512]{3,2,1,0:T(8,128)(2,1)} %bitcast.64, f32[2,256]{1,0:T(2,128)S(1)} %compare_convert_fusion), kind=kOutput, calls=%fused_computation.14 | convolution fusion | flops 33619968 | bytes 722944 | tf_op jit(solution)/shard_map/tbr,tbc->trc/dot_general | solution.py:53
  9.4 0.8 broadcast_in_dim.2
  10.2 11.5 %all-to-all-start = ((bf16[8,2,256,64]{2,3,1,0:T(8,128)(2,1)}), bf16[8,2,256,64]{2,3,1,0:T(8,128)(2,1)S(1)}, u32[]{:S(2)}, u32[]{:S(2)}) async-start(bf16[8,2,256,64]{2,3,1,0:T(8,128)(2,1)} %broadcast_in_dim.2), calls=%async_computation | async-start | bytes 1048576 | tf_op jit(solution)/shard_map/all_to_all | solution.py:16
  21.7 0.0 all-gather.2.cloned.1.call-start
  21.7 0.7 fusion.16
  22.4 0.0 copy-done
  22.4 1.1 fusion.10
  23.5 0.6 copy.17
  24.2 0.0 all-gather.2.cloned.1.call-update
  24.2 9.1 %all-to-all-done = bf16[8,2,256,64]{2,3,1,0:T(8,128)(2,1)S(1)} async-done(((bf16[8,2,256,64]{2,3,1,0:T(8,128)(2,1)}), bf16[8,2,256,64]{2,3,1,0:T(8,128)(2,1)S(1)}, u32[]{:S(2)}, u32[]{:S(2)}) %all-to-all-start) | async-done | bytes 524320 | tf_op jit(solution)/shard_map/all_to_all | solution.py:16
  33.3 1.6 %stack.2 = bf16[32,16,512]{2,1,0:T(8,128)(2,1)} broadcast(bf16[16,512]{1,0:T(8,128)(2,1)} %param.18), dimensions={1,2} | broadcast | bytes 540672 | tf_op jit(solution)/shard_map/stack | solution.py:9
  34.9 13.8 %all-to-all-start.1 = ((bf16[32,16,512]{2,1,0:T(8,128)(2,1)}), bf16[32,16,512]{2,1,0:T(8,128)(2,1)S(1)}, u32[]{:S(2)}, u32[]{:S(2)}) async-start(bf16[32,16,512]{2,1,0:T(8,128)(2,1)} %stack.2), calls=%async_computation.1 | async-start | bytes 1048576 | tf_op jit(solution)/shard_map/all_to_all | solution.py:10
  48.6 0.8 copy.19
  49.5 15.6 %all-to-all-done.1 = bf16[32,16,512]{2,1,0:T(8,128)(2,1)S(1)} async-done(((bf16[32,16,512]{2,1,0:T(8,128)(2,1)}), bf16[32,16,512]{2,1,0:T(8,128)(2,1)S(1)}, u32[]{:S(2)}, u32[]{:S(2)}) %all-to-all-start.1) | async-done | bytes 524320 | tf_op jit(solution)/shard_map/all_to_all | solution.py:10
  65.1 0.0 copy-done.2
  65.1 1.2 fusion.6
  66.3 2.2 %fusion.7 = f32[2,512,512]{1,2,0:T(8,128)S(1)} fusion(bf16[2,512,256]{2,1,0:T(8,128)(2,1)} %bitcast.59, bf16[2,256,512]{1,2,0:T(8,128)(2,1)} %bitcast.61, bf16[512,512,1]{1,0,2:T(8,128)(2,1)} %fusion.6), kind=kOutput, calls=%fused_computation.12 | convolution fusion | flops 537133056 | bytes 3670016 | tf_op jit(solution)/shard_map/ibr,irg->ibg/dot_general | solution.py:79
  68.5 2.7 %fusion = bf16[1024,512]{1,0:T(8,128)(2,1)} fusion(f32[2,512,512]{1,2,0:T(8,128)S(1)} %fusion.7, bf16[1024,512]{1,0:T(8,128)(2,1)} %param.19), kind=kLoop, calls=%fused_computation.3 | loop fusion | flops 1572864 | bytes 4194304 | tf_op jit(solution)/shard_map/convert_element_type | solution.py:81
  71.2 16.0 %all-gather.2.cloned.1.call-done = bf16[512,4,256]{2,1,0:T(4,128)(2,1)} async-done(((bf16[16,4,256]{2,1,0:T(4,128)(2,1)}), bf16[512,4,256]{2,1,0:T(4,128)(2,1)}) %all-gather.2.cloned.1.call-update) | async-done | bytes 1048592 | tf_op jit(solution)/shard_map/all_gather | solution.py:62
  87.2 2.1 %fusion.5 = bf16[2,4,256,256]{2,3,0,1:T(8,128)(2,1)S(1)} fusion(bf16[2,256,512,1]{1,2,0,3:T(8,128)(2,1)} %bitcast.62, bf16[512,4,256,1]{2,1,0,3:T(4,128)(2,1)} %bitcast.66), kind=kOutput, calls=%fused_computation.8 | convolution fusion | flops 537395200 | bytes 2621440 | tf_op jit(solution)/shard_map/irp,pjs->ijrs/dot_general | solution.py:66
  89.3 6.1 %convolution_bitcast_fusion = f32[2,512,4,512]{3,1,0,2:T(8,128)} fusion(bf16[4,512,256,1]{2,1,3,0:T(8,128)(2,1)S(1)} %bitcast.54, bf16[2,4,256,256]{2,3,0,1:T(8,128)(2,1)S(1)} %fusion.5, bf16[2,512,256,1]{2,1,0,3:T(8,128)(2,1)} %bitcast.60), kind=kOutput, calls=%fused_computation.1 | convolution fusion | flops 1611661312 | bytes 11010048 | tf_op jit(solution)/shard_map/ijbs,jcs->ibjc/dot_general | solution.py:72
  95.4 12.0 %copy.23 = f32[2,512,4,512]{3,2,1,0:T(4,128)} copy(f32[2,512,4,512]{3,1,0,2:T(8,128)} %convolution_bitcast_fusion) | data formatting | bytes 16777216 | tf_op jit(solution)/shard_map/ijbs,jcs->ibjc/transpose | solution.py:72
  107.4 0.0 copy-start.1
  107.4 7.8 %copy.35 = f32[128,8,4,512]{3,1,2,0:T(8,128)S(1)} copy(f32[128,8,4,512]{3,2,1,0:T(4,128)} %bitcast.56) | data formatting | bytes 16777216
  115.3 0.0 copy-done.1
  115.3 3.5 %subtract_convert_fusion = bf16[1024,2048]{1,0:T(8,128)(2,1)} fusion(f32[1024,2048]{1,0:T(8,128)S(1)} %bitcast.57, bf16[1024,2048]{1,0:T(8,128)(2,1)S(1)} %copy-done.1), kind=kLoop, calls=%fused_computation | loop fusion | flops 6291456 | bytes 16777216 | tf_op jit(solution)/shard_map/convert_element_type | solution.py:74
Async XLA Ops:
  7.2 15.3 %copy-start = (bf16[2048,256]{1,0:T(8,128)(2,1)S(1)}, bf16[2048,256]{1,0:T(8,128)(2,1)}, u32[]{:S(2)}) copy-start(bf16[2048,256]{1,0:T(8,128)(2,1)} %param.14) | copy-start | bytes 3145732
  7.2 57.9 %copy-start.2 = (bf16[512,512]{1,0:T(8,128)(2,1)S(1)}, bf16[512,512]{1,0:T(8,128)(2,1)}, u32[]{:S(2)}) copy-start(bf16[512,512]{1,0:T(8,128)(2,1)} %param.17) | copy-start | bytes 1572868
  10.2 23.1 %all-to-all-start = ((bf16[8,2,256,64]{2,3,1,0:T(8,128)(2,1)}), bf16[8,2,256,64]{2,3,1,0:T(8,128)(2,1)S(1)}, u32[]{:S(2)}, u32[]{:S(2)}) async-start(bf16[8,2,256,64]{2,3,1,0:T(8,128)(2,1)} %broadcast_in_dim.2), calls=%async_computation | async-start | bytes 1048576 | tf_op jit(solution)/shard_map/all_to_all | solution.py:16
  21.7 65.5 %all-gather.2.cloned.1.call-start = ((), (), s32[]{:S(2)}) async-start(), calls=%async_computation.2 | async-start | bytes 1081344 | tf_op jit(solution)/shard_map/all_gather | solution.py:62
  34.9 30.2 %all-to-all-start.1 = ((bf16[32,16,512]{2,1,0:T(8,128)(2,1)}), bf16[32,16,512]{2,1,0:T(8,128)(2,1)S(1)}, u32[]{:S(2)}, u32[]{:S(2)}) async-start(bf16[32,16,512]{2,1,0:T(8,128)(2,1)} %stack.2), calls=%async_computation.1 | async-start | bytes 1048576 | tf_op jit(solution)/shard_map/all_to_all | solution.py:10
  107.4 7.9 %copy-start.1 = (bf16[1024,2048]{1,0:T(8,128)(2,1)S(1)}, bf16[1024,2048]{1,0:T(8,128)(2,1)}, u32[]{:S(2)}) copy-start(bf16[1024,2048]{1,0:T(8,128)(2,1)} %param.10) | copy-start | bytes 12582916
Sparse Core Ops, SparseCore 0:
  24.3 62.8 all-gather.1
